TPU v7x, 32 devices: a whole 2x2x4 slice. The times are simulated.
32 devices in a mesh: dp: 4 (over z), expert: 8 (over y, x, core).
Axes of the slice: x: 2, y: 2, z: 4, core: 2. Of those that a mesh axis runs over, the one named last changes fastest.
Arguments:
- tokens: bfloat16 [4096, 4096], P(('dp', 'expert')), may hold values from -6 to 6
- chosen: int32 [32, 128], replicated, may hold values from 0 to 4095, as said below
- gate_levels: int32 [32, 128], replicated, may hold values from 32 to 255
- expert_gate: bfloat16 [32, 4096, 768], P(('dp', 'expert')), may hold values from -0.09375 to 0.09375
- expert_up: bfloat16 [32, 4096, 768], P(('dp', 'expert')), may hold values from -0.09375 to 0.09375
- expert_down: bfloat16 [32, 768, 4096], P(('dp', 'expert')), may hold values from -0.21875 to 0.21875
- shared_gate: bfloat16 [4096, 4096], P(('dp', 'expert')), may hold values from -0.09375 to 0.09375
- shared_up: bfloat16 [4096, 4096], P(('dp', 'expert')), may hold values from -0.09375 to 0.09375
- shared_down: bfloat16 [4096, 4096], P(('dp', 'expert')), may hold values from -0.09375 to 0.09375
Outputs:
- block_out: bfloat16 [4096, 4096], P(('dp', 'expert'))
Inputs may be any that keep to these rules, and one draw needn't show every extreme that they name: `chosen`: token t lies in the rows of device t // 128 (devices numbered dp-major). Each expert's 128 indices are different; at most 8 of them lie in the rows of one device, and for every expert some device gives exactly 8.
All inputs are finite; a program needn't handle non-finite values.
Results may differ from a plain program's by a relative error of at most 0.0052.
Values may be sent and summed in bfloat16 or wider, within the bound.
A program may use at most 128 MiB of HBM per device.

v0:
```python
import jax
import jax.numpy as jnp
from jax import lax
from jax.sharding import PartitionSpec as P


def expert_rows(rows, w_gate, w_up, w_down):
    gated = jnp.dot(rows, w_gate, preferred_element_type=jnp.float32)
    lifted = jnp.dot(rows, w_up, preferred_element_type=jnp.float32)
    hidden = (jax.nn.silu(gated) * lifted).astype(jnp.bfloat16)
    return jnp.dot(hidden, w_down, preferred_element_type=jnp.float32).astype(jnp.bfloat16)


def slot_tables(levels, wanted, start_positions, slot_total, row_total):
    ranking = jnp.cumsum(wanted.astype(jnp.int32), axis=1) - 1
    slot_ids = jnp.arange(slot_total, dtype=jnp.int32)
    picks = wanted[:, :, None] & (ranking[:, :, None] == slot_ids[None, None, :])
    row_index = jnp.sum(jnp.where(picks, start_positions[:, :, None], 0), axis=1).reshape(-1)
    filled = jnp.any(picks, axis=1).reshape(-1)
    capacity_gating_weight = jnp.sum(jnp.where(picks, levels[:, :, None], 0.0), axis=1).reshape(-1)
    row_ids = jnp.arange(row_total, dtype=jnp.int32)
    member = (row_index[None, :] == row_ids[:, None]) & filled[None, :]
    selector = member.astype(jnp.bfloat16)
    weighted = jnp.where(member, capacity_gating_weight[None, :], 0.0).astype(jnp.bfloat16)
    return (selector, weighted)


def local(
    tokens,
    chosen,
    gate_levels,
    expert_gate,
    expert_up,
    expert_down,
    shared_gate,
    shared_up,
    shared_down,
):
    n_data = lax.axis_size("dp")
    n_expert = lax.axis_size("expert")
    accelerator_roster = n_data * n_expert
    tok_dev = tokens.shape[0]
    width = tokens.shape[1]
    slot_most = 2 * tok_dev // accelerator_roster
    row_data = lax.axis_index("dp")
    row_expert = lax.axis_index("expert")
    multiplier_factors = gate_levels.astype(jnp.float32) / 256.0
    pick_rows = (((0,), (0,)), ((), ()))
    contract = (((1,), (1,)), ((), ()))
    column = lax.all_gather(tokens, "dp", axis=0, tiled=True)
    gate_rows, up_rows, down_rows = (
        lax.all_gather(shared_gate, "expert", axis=0, tiled=True),
        lax.all_gather(shared_up, "expert", axis=0, tiled=True),
        lax.all_gather(shared_down, "expert", axis=0, tiled=True),
    )
    gated = lax.dot_general(column, gate_rows, contract, preferred_element_type=jnp.float32)
    lifted = lax.dot_general(column, up_rows, contract, preferred_element_type=jnp.float32)
    shared_hidden = (jax.nn.silu(gated) * lifted).astype(jnp.bfloat16)
    routed_own = None
    myself = row_data * n_expert + row_expert
    wanted = chosen // tok_dev == myself
    selector, weighted = slot_tables(
        multiplier_factors, wanted, chosen % tok_dev, slot_most, tok_dev
    )
    outgoing = lax.dot_general(selector, tokens, pick_rows, preferred_element_type=jnp.float32)
    outgoing, weighted = (outgoing.astype(jnp.bfloat16), weighted)
    outgoing = outgoing.reshape(accelerator_roster, slot_most, width)
    received = lax.all_to_all(outgoing, ("dp", "expert"), split_axis=0, concat_axis=0, tiled=True)
    flat = received.reshape(-1, width)
    returned = lax.all_to_all(
        expert_rows(flat, expert_gate[0], expert_up[0], expert_down[0]).reshape(received.shape),
        ("dp", "expert"),
        split_axis=0,
        concat_axis=0,
        tiled=True,
    )
    routed_own = jnp.dot(weighted, returned.reshape(-1, width), preferred_element_type=jnp.float32)
    value = jnp.dot(shared_hidden, down_rows, preferred_element_type=jnp.float32)
    combined = lax.psum_scatter(value, "dp", scatter_dimension=0, tiled=True)
    combined = combined + routed_own
    return combined.astype(jnp.bfloat16)


def solution(mesh):
    placed = (
        P(("dp", "expert"), None),
        P(),
        P(),
        P(("dp", "expert"), None, None),
        P(("dp", "expert"), None, None),
        P(("dp", "expert"), None, None),
        P(("dp", "expert"), None),
        P(("dp", "expert"), None),
        P(("dp", "expert"), None),
    )
    return jax.shard_map(
        local, mesh=mesh, in_specs=placed, out_specs=P(("dp", "expert"), None), check_vma=False
    )
```

profile of v0, /device:TPU:9, one launch (start us, length us, event | category | flops | bytes accessed | tf_op | source)
XLA Modules:
  0.0 521.2 jit_solution(7123957170573335426)
XLA Ops:
  6.5 0.7 all-gather.5.cloned.1.call-update
  7.3 0.7 all-gather.7.cloned.1.call-update
  8.1 0.7 all-gather.11.cloned.1.call-update
  8.8 0.5 all-gather.9.cloned.1.call-update
  9.4 79.0 %all-gather.5.cloned.1.call-done = bf16[512,4096]{1,0:T(8,128)(2,1)} async-done(((bf16[128,4096]{1,0:T(8,128)(2,1)}), bf16[512,4096]{1,0:T(8,128)(2,1)}) %all-gather.5.cloned.1.call-update) | async-done | bytes 4194320 | tf_op jit(solution)/shard_map/all_gather | solution.py:50
  88.4 57.8 %all-gather.7.cloned.1.call-done = bf16[1024,4096]{1,0:T(8,128)(2,1)} async-done(((bf16[128,4096]{1,0:T(8,128)(2,1)}), bf16[1024,4096]{1,0:T(8,128)(2,1)}) %all-gather.7.cloned.1.call-update) | async-done | bytes 8388624 | tf_op jit(solution)/shard_map/all_gather | solution.py:52
  146.1 8.2 %fusion.49 = f32[512,1024]{1,0:T(8,128)S(1)} fusion(bf16[512,4096]{1,0:T(8,128)(2,1)} %all-gather.5.cloned.1.call-done, bf16[1024,4096]{1,0:T(8,128)(2,1)} %all-gather.7.cloned.1.call-done), kind=kOutput, calls=%fused_computation.47 | convolution fusion | flops 4294967296 | bytes 14680064 | tf_op jit(solution)/shard_map/dot_general | solution.py:56
  154.4 48.1 %all-gather.11.cloned.1.call-done = bf16[1024,4096]{1,0:T(8,128)(2,1)} async-done(((bf16[128,4096]{1,0:T(8,128)(2,1)}), bf16[1024,4096]{1,0:T(8,128)(2,1)}) %all-gather.11.cloned.1.call-update) | async-done | bytes 8388624 | tf_op jit(solution)/shard_map/all_gather | solution.py:54
  202.5 56.2 %all-gather.9.cloned.1.call-done = bf16[1024,4096]{1,0:T(8,128)(2,1)} async-done(((bf16[128,4096]{1,0:T(8,128)(2,1)}), bf16[1024,4096]{1,0:T(8,128)(2,1)}) %all-gather.9.cloned.1.call-update) | async-done | bytes 8388624 | tf_op jit(solution)/shard_map/all_gather | solution.py:53
  258.6 19.1 %fusion.50 = f32[512,4096]{1,0:T(8,128)} fusion(bf16[1024,4096]{1,0:T(8,128)(2,1)} %all-gather.11.cloned.1.call-done, f32[512,1024]{1,0:T(8,128)S(1)} %fusion.49, bf16[512,4096]{1,0:T(8,128)(2,1)} %all-gather.5.cloned.1.call-done, bf16[1024,4096]{1,0:T(8,128)(2,1)} %all-gather.9.cloned.1.call-done), kind=kOutput, calls=%fused_computation.48 | convolution fusion | flops 8593080320 | bytes 31457280 | tf_op jit(solution)/shard_map/dot_general | solution.py:78
  277.8 0.7 copy-done.1
  278.5 0.3 reduce_window_sum.11
  278.8 0.6 select_reduce_fusion.1
  279.5 0.6 fusion.33
  280.1 0.1 and.34
  280.3 0.8 fusion.12
  281.0 106.4 %all_to_all.10 = bf16[32,8,4096]{2,1,0:T(8,128)(2,1)S(1)} all-to-all(bf16[32,8,4096]{2,1,0:T(8,128)(2,1)S(1)} %fusion.12), channel_id=1, replica_groups=mesh['dp'=4,'expert'=8] {'dp','expert'}, dimensions={0} | all-to-all | bytes 4194304 | tf_op jit(solution)/shard_map/all_to_all | solution.py:68
  387.4 4.6 fusion.4
  392.0 10.8 %fusion.9 = bf16[32,8,4096]{2,1,0:T(8,128)(2,1)} fusion(bf16[1,768,4096]{2,1,0:T(8,128)(2,1)} %param.14, bf16[1,4096,768]{2,1,0:T(8,128)(2,1)} %param.13, bf16[32,8,4096]{2,1,0:T(8,128)(2,1)S(1)} %all_to_all.10, f32[256,768]{1,0:T(8,128)S(1)} %fusion.4), kind=kOutput, calls=%fused_computation.8 | convolution fusion | flops 3223453696 | bytes 17563648 | tf_op jit(solution)/shard_map/dot_general | solution.py:11
  402.8 6.9 %all-to-all-start.1 = ((bf16[32,8,4096]{2,1,0:T(8,128)(2,1)}), bf16[32,8,4096]{2,1,0:T(8,128)(2,1)S(1)}, u32[]{:S(2)}, u32[]{:S(2)}) async-start(bf16[32,8,4096]{2,1,0:T(8,128)(2,1)} %fusion.9), calls=%async_computation.2 | async-start | bytes 4194304 | tf_op jit(solution)/shard_map/all_to_all | solution.py:70
  409.8 0.1 select_reduce_fusion
  410.0 90.3 %all-to-all-done.1 = bf16[32,8,4096]{2,1,0:T(8,128)(2,1)S(1)} async-done(((bf16[32,8,4096]{2,1,0:T(8,128)(2,1)}), bf16[32,8,4096]{2,1,0:T(8,128)(2,1)S(1)}, u32[]{:S(2)}, u32[]{:S(2)}) %all-to-all-start.1) | async-done | bytes 2097184 | tf_op jit(solution)/shard_map/all_to_all | solution.py:70
  500.2 11.4 %reduce-scatter.2.cloned.1.call-done = f32[128,4096]{1,0:T(8,128)} async-done(((f32[512,4096]{1,0:T(8,128)}), f32[128,4096]{1,0:T(8,128)}) %reduce-scatter.2.cloned.1.call-update) | async-done | bytes 2097168 | tf_op jit(solution)/shard_map/reduce_scatter | solution.py:79
  511.6 3.1 fusion.13
  (16 shorter events, 0.4 us)
Async XLA Ops:
  6.5 81.8 %all-gather.5.cloned.1.call-start = ((), (), s32[]{:S(2)}) async-start(), calls=%async_computation.3 | async-start | bytes 5242880 | tf_op jit(solution)/shard_map/all_gather | solution.py:50
  7.3 138.9 %all-gather.7.cloned.1.call-start = ((), (), s32[]{:S(2)}) async-start(), calls=%async_computation.4 | async-start | bytes 9437184 | tf_op jit(solution)/shard_map/all_gather | solution.py:52
  8.0 194.5 %all-gather.11.cloned.1.call-start = ((), (), s32[]{:S(2)}) async-start(), calls=%async_computation.6 | async-start | bytes 9437184 | tf_op jit(solution)/shard_map/all_gather | solution.py:54
  8.7 249.9 %all-gather.9.cloned.1.call-start = ((), (), s32[]{:S(2)}) async-start(), calls=%async_computation.5 | async-start | bytes 9437184 | tf_op jit(solution)/shard_map/all_gather | solution.py:53
  9.3 502.3 %reduce-scatter.2.cloned.1.call-start = ((), (), s32[]{:S(2)}) async-start(), calls=%async_computation.7 | async-start | bytes 10485760 | tf_op jit(solution)/shard_map/reduce_scatter | solution.py:79
  277.8 0.7 copy-start.1
  277.8 2.5 copy-start
  402.8 7.0 %copy-start.2 = (s32[32,128]{1,0:T(8,128)S(1)}, s32[32,128]{1,0:T(8,128)}, u32[]{:S(2)}) copy-start(s32[32,128]{1,0:T(8,128)} %param.11) | copy-start | bytes 49156
  402.8 97.5 %all-to-all-start.1 = ((bf16[32,8,4096]{2,1,0:T(8,128)(2,1)}), bf16[32,8,4096]{2,1,0:T(8,128)(2,1)S(1)}, u32[]{:S(2)}, u32[]{:S(2)}) async-start(bf16[32,8,4096]{2,1,0:T(8,128)(2,1)} %fusion.9), calls=%async_computation.2 | async-start | bytes 4194304 | tf_op jit(solution)/shard_map/all_to_all | solution.py:70
Sparse Core Ops, SparseCore 0:
  8.9 79.3 all-gather.4
  90.2 55.8 all-gather.6
  148.0 54.3 all-gather.10
  204.2 54.3 all-gather.8
  277.9 233.6 reduce-scatter.1
where the time goes:
time: 522 us; the launch traced here: 521 us
  waiting for transfers between devices  345 us (66%)
  blocking collectives  106 us (20%)
  matrix products  46.6 us (9%)
  between operations  13.2 us (3%)
  starting transfers between devices  7.1 us (1%)
    all_to_all x1, blocking collectives, local(): lax.all_to_all(outgoing, ('dp', 'expert'), split_axis=0, concat_axis=0, t...  106 us
    all_to_all x1, waiting for transfers between devices, local(): lax.all_to_all(expert_rows(flat, expert_gate[0], expert_up[0], expert_dow...  90.3 us
    all_gather x1, waiting for transfers between devices, local(): column = lax.all_gather(tokens, 'dp', axis=0, tiled=True)  79 us
    all_gather x1, waiting for transfers between devices, local(): lax.all_gather(shared_gate, 'expert', axis=0, tiled=True)  57.8 us
    all_gather x1, waiting for transfers between devices, local(): lax.all_gather(shared_up, 'expert', axis=0, tiled=True)  56.2 us
    all_gather x1, waiting for transfers between devices, local(): lax.all_gather(shared_down, 'expert', axis=0, tiled=True)  48.1 us
    dot_general x1, matrix products, local(): jnp.dot(shared_hidden, down_rows, preferred_element_type=jnp.float32)  19.1 us
    reduce_scatter x1, waiting for transfers between devices, local(): combined = lax.psum_scatter(value, 'dp', scatter_dimension=0, tiled=True)  11.4 us
  transfers between devices with their start and end apart: 6, of which 6 were waited for; matrix products, arithmetic and copies ran while one was open for 5% of the time, Pallas kernels for 0%

commit v1 on v0

--- a/solution.py
+++ b/solution.py
@@ -2,6 +2,16 @@
 import jax.numpy as jnp
 from jax import lax
 from jax.sharding import PartitionSpec as P
+
+
+def turned_line(value, axis, dim):
+    count = lax.axis_size(axis)
+    held, pieces = (value, [value])
+    for _ in range(count - 1):
+        held = lax.ppermute(held, axis, [(i, (i + 1) % count) for i in range(count)])
+        pieces.insert(0, held)
+    line = jnp.concatenate(pieces, axis=dim)
+    return jnp.roll(line, (lax.axis_index(axis) + 1) * value.shape[dim], axis=dim)
 
 
 def expert_rows(rows, w_gate, w_up, w_down):
@@ -47,7 +57,7 @@
     multiplier_factors = gate_levels.astype(jnp.float32) / 256.0
     pick_rows = (((0,), (0,)), ((), ()))
     contract = (((1,), (1,)), ((), ()))
-    column = lax.all_gather(tokens, "dp", axis=0, tiled=True)
+    column = turned_line(tokens, "dp", 0)
     gate_rows, up_rows, down_rows = (
         lax.all_gather(shared_gate, "expert", axis=0, tiled=True),
         lax.all_gather(shared_up, "expert", axis=0, tiled=True),

time: 522 us -> 441 us (0.84)
  waiting for transfers between devices: 345 us -> 250 us
  local copies, waits for them, and re-layouts: 0.99 us -> 12.1 us
    all_gather x1 -> x0, waiting for transfers between devices: 79 us -> none  [local(): column = lax.all_gather(tokens, 'dp', axis=0, tiled=True)]
    ppermute x0 -> x3, waiting for transfers between devices: none -> 70.7 us  [turned_line(): lax.ppermute(held, axis, [(i, (i + 1) % count) for i in range(count)])]
    all_gather x1, waiting for transfers between devices: 56.2 us -> 0.01 us  [local(): lax.all_gather(shared_up, 'expert', axis=0, tiled=True)]
    all_gather x1, waiting for transfers between devices: 57.8 us -> 19 us  [local(): lax.all_gather(shared_gate, 'expert', axis=0, tiled=True)]
    unnamed x6 -> x13, local copies, waits for them, and re-layouts: 0.69 us -> 10.7 us
    all_gather x1, waiting for transfers between devices: 48.1 us -> 56.3 us  [local(): lax.all_gather(shared_down, 'expert', axis=0, tiled=True)]
  transfers between devices with their start and end apart: 6 -> 8, of which waited for: 6 -> 7; matrix products, arithmetic and copies ran while one was open for 5% -> 9% of each run, Pallas kernels for 0% -> 0%
where the time goes in v1:
time: 441 us
  waiting for transfers between devices  250 us (57%)
  blocking collectives  106 us (24%)
  matrix products  47.8 us (11%)
  between operations  13.2 us (3%)
  local copies, waits for them, and re-layouts  12.1 us (3%)
  starting transfers between devices  9.62 us (2%)
    all_to_all x1, blocking collectives, local(): lax.all_to_all(outgoing, ('dp', 'expert'), split_axis=0, concat_axis=0, t...  106 us
    all_to_all x1, waiting for transfers between devices, local(): lax.all_to_all(expert_rows(flat, expert_gate[0], expert_up[0], expert_dow...  90.3 us
    ppermute x3, waiting for transfers between devices, turned_line(): lax.ppermute(held, axis, [(i, (i + 1) % count) for i in range(count)])  70.7 us
    all_gather x1, waiting for transfers between devices, local(): lax.all_gather(shared_down, 'expert', axis=0, tiled=True)  56.3 us
    dot_general x1, matrix products, local(): jnp.dot(shared_hidden, down_rows, preferred_element_type=jnp.float32)  19.3 us
    all_gather x1, waiting for transfers between devices, local(): lax.all_gather(shared_gate, 'expert', axis=0, tiled=True)  19 us
    reduce_scatter x1, waiting for transfers between devices, local(): combined = lax.psum_scatter(value, 'dp', scatter_dimension=0, tiled=True)  11.4 us
    dot_general x1, matrix products, expert_rows(): jnp.dot(hidden, w_down, preferred_element_type=jnp.float32)  10.8 us
  transfers between devices with their start and end apart: 8, of which 7 were waited for; matrix products, arithmetic and copies ran while one was open for 9% of the time, Pallas kernels for 0%

profile of v1, /device:TPU:9, one launch (start us, length us, event | category | flops | bytes accessed | tf_op | source)
XLA Modules:
  0.0 440.6 jit_solution(18011239342145070861)
XLA Ops:
  8.8 1.3 collective-permute-start
  10.1 23.0 %collective-permute-done = bf16[128,4096]{1,0:T(8,128)(2,1)S(1)} collective-permute-done((bf16[128,4096]{1,0:T(8,128)(2,1)}, bf16[128,4096]{1,0:T(8,128)(2,1)S(1)}, u32[]{:S(2)}, u32[]{:S(2)}) %collective-permute-start) | collective-permute-done | bytes 1048608 | tf_op jit(solution)/shard_map/ppermute | solution.py:11
  33.2 1.2 collective-permute-start.1
  34.4 23.4 %collective-permute-done.1 = bf16[128,4096]{1,0:T(8,128)(2,1)S(1)} collective-permute-done((bf16[128,4096]{1,0:T(8,128)(2,1)S(1)}, bf16[128,4096]{1,0:T(8,128)(2,1)S(1)}, u32[]{:S(2)}, u32[]{:S(2)}) %collective-permute-start.1) | collective-permute-done | bytes 1048608 | tf_op jit(solution)/shard_map/ppermute | solution.py:11
  57.8 24.3 %collective-permute-done.2 = bf16[128,4096]{1,0:T(8,128)(2,1)} collective-permute-done((bf16[128,4096]{1,0:T(8,128)(2,1)S(1)}, bf16[128,4096]{1,0:T(8,128)(2,1)}, u32[]{:S(2)}, u32[]{:S(2)}) %collective-permute-start.2) | collective-permute-done | bytes 1048608 | tf_op jit(solution)/shard_map/ppermute | solution.py:11
  82.1 2.4 constant_dynamic-update-slice_fusion.7
  84.4 1.0 constant_dynamic-update-slice_fusion.6
  85.5 1.0 constant_dynamic-update-slice_fusion.5
  86.5 1.1 constant_dynamic-update-slice_fusion.4
  87.6 2.4 constant_dynamic-update-slice_fusion.3
  90.0 1.0 constant_dynamic-update-slice_fusion.2
  91.0 1.1 constant_dynamic-update-slice_fusion.1
  92.1 1.1 constant_dynamic-update-slice_fusion
  93.2 9.4 %fusion.14 = f32[512,1024]{1,0:T(8,128)S(1)} fusion(bf16[1024,4096]{1,0:T(8,128)(2,1)} %all-gather.6.cloned.1.call-done, bf16[1024,4096]{1,0:T(8,128)(2,1)} %constant_dynamic-update-slice_fusion, s32[]{:T(128)S(6)} %select_n.37), kind=kOutput, calls=%fused_computation.12 | convolution fusion | flops 4294967296 | bytes 14680068 | tf_op jit(solution)/shard_map/dot_general | solution.py:67
  102.6 19.0 %all-gather.4.cloned.1.call-done = bf16[1024,4096]{1,0:T(8,128)(2,1)} async-done(((bf16[128,4096]{1,0:T(8,128)(2,1)}), bf16[1024,4096]{1,0:T(8,128)(2,1)}) %all-gather.4.cloned.1.call-update) | async-done | bytes 8388624 | tf_op jit(solution)/shard_map/all_gather | solution.py:62
  121.6 56.3 %all-gather.8.cloned.1.call-done = bf16[1024,4096]{1,0:T(8,128)(2,1)} async-done(((bf16[128,4096]{1,0:T(8,128)(2,1)}), bf16[1024,4096]{1,0:T(8,128)(2,1)}) %all-gather.8.cloned.1.call-update) | async-done | bytes 8388624 | tf_op jit(solution)/shard_map/all_gather | solution.py:64
  177.9 19.3 %fusion.31 = f32[512,4096]{1,0:T(8,128)} fusion(bf16[1024,4096]{1,0:T(8,128)(2,1)} %all-gather.8.cloned.1.call-done, f32[512,1024]{1,0:T(8,128)S(1)} %fusion.14, bf16[1024,4096]{1,0:T(8,128)(2,1)} %all-gather.4.cloned.1.call-done, bf16[1024,4096]{1,0:T(8,128)(2,1)} %constant_dynamic-update-slice_fusion, s32[]{:T(128)S(6)} %select_n.37), kind=kOutput, calls=%fused_computation.22 | convolution fusion | flops 8593080320 | bytes 31457284 | tf_op jit(solution)/shard_map/dot_general | solution.py:88
  200.4 106.4 %all_to_all.10 = bf16[32,8,4096]{2,1,0:T(8,128)(2,1)S(1)} all-to-all(bf16[32,8,4096]{2,1,0:T(8,128)(2,1)S(1)} %fusion.12), channel_id=1, replica_groups=mesh['dp'=4,'expert'=8] {'dp','expert'}, dimensions={0} | all-to-all | bytes 4194304 | tf_op jit(solution)/shard_map/all_to_all | solution.py:78
  306.8 4.6 %fusion.4 = f32[256,768]{1,0:T(8,128)S(1)} fusion(bf16[1,4096,768]{2,1,0:T(8,128)(2,1)} %param.12, bf16[32,8,4096]{2,1,0:T(8,128)(2,1)S(1)} %all_to_all.10), kind=kOutput, calls=%fused_computation.4 | convolution fusion | flops 1610612736 | bytes 9175040 | tf_op jit(solution)/shard_map/dot_general | solution.py:18
  311.4 10.8 %fusion.9 = bf16[32,8,4096]{2,1,0:T(8,128)(2,1)} fusion(bf16[1,768,4096]{2,1,0:T(8,128)(2,1)} %param.14, bf16[1,4096,768]{2,1,0:T(8,128)(2,1)} %param.13, bf16[32,8,4096]{2,1,0:T(8,128)(2,1)S(1)} %all_to_all.10, f32[256,768]{1,0:T(8,128)S(1)} %fusion.4), kind=kOutput, calls=%fused_computation.8 | convolution fusion | flops 3223453696 | bytes 17563648 | tf_op jit(solution)/shard_map/dot_general | solution.py:21
  322.2 6.9 %all-to-all-start.1 = ((bf16[32,8,4096]{2,1,0:T(8,128)(2,1)}), bf16[32,8,4096]{2,1,0:T(8,128)(2,1)S(1)}, u32[]{:S(2)}, u32[]{:S(2)}) async-start(bf16[32,8,4096]{2,1,0:T(8,128)(2,1)} %fusion.9), calls=%async_computation.2 | async-start | bytes 4194304 | tf_op jit(solution)/shard_map/all_to_all | solution.py:80
  329.4 90.3 %all-to-all-done.1 = bf16[32,8,4096]{2,1,0:T(8,128)(2,1)S(1)} async-done(((bf16[32,8,4096]{2,1,0:T(8,128)(2,1)}), bf16[32,8,4096]{2,1,0:T(8,128)(2,1)S(1)}, u32[]{:S(2)}, u32[]{:S(2)}) %all-to-all-start.1) | async-done | bytes 2097184 | tf_op jit(solution)/shard_map/all_to_all | solution.py:80
  419.6 11.4 %reduce-scatter.2.cloned.1.call-done = f32[128,4096]{1,0:T(8,128)} async-done(((f32[512,4096]{1,0:T(8,128)}), f32[128,4096]{1,0:T(8,128)}) %reduce-scatter.2.cloned.1.call-update) | async-done | bytes 2097168 | tf_op jit(solution)/shard_map/reduce_scatter | solution.py:89
  431.0 3.1 fusion.13
  (28 shorter events, 5.7 us)
Async XLA Ops:
  6.5 80.0 %copy-start = (bf16[128,4096]{1,0:T(8,128)(2,1)S(1)}, bf16[128,4096]{1,0:T(8,128)(2,1)}, u32[]{:S(2)}) copy-start(bf16[128,4096]{1,0:T(8,128)(2,1)} %param.9) | copy-start | bytes 3145732
  6.5 86.7 %all-gather.6.cloned.1.call-start = ((), (), s32[]{:S(2)}) async-start(), calls=%async_computation.4 | async-start | bytes 9437184 | tf_op jit(solution)/shard_map/all_gather | solution.py:63
  7.3 114.3 %all-gather.4.cloned.1.call-start = ((), (), s32[]{:S(2)}) async-start(), calls=%async_computation.3 | async-start | bytes 9437184 | tf_op jit(solution)/shard_map/all_gather | solution.py:62
  8.0 169.9 %all-gather.8.cloned.1.call-start = ((), (), s32[]{:S(2)}) async-start(), calls=%async_computation.5 | async-start | bytes 9437184 | tf_op jit(solution)/shard_map/all_gather | solution.py:64
  8.7 422.3 %reduce-scatter.2.cloned.1.call-start = ((), (), s32[]{:S(2)}) async-start(), calls=%async_computation.6 | async-start | bytes 10485760 | tf_op jit(solution)/shard_map/reduce_scatter | solution.py:89
  8.8 24.4 %collective-permute-start = (bf16[128,4096]{1,0:T(8,128)(2,1)}, bf16[128,4096]{1,0:T(8,128)(2,1)S(1)}, u32[]{:S(2)}, u32[]{:S(2)}) collective-permute-start(bf16[128,4096]{1,0:T(8,128)(2,1)} %param.9), channel_id=1, source_target_pairs={{0,8},{8,16},{16,24},{24,0},{1,9},{9,17},{17,25},{25,1},{2,10},{10... | collective-permute-start | bytes 3145736 | tf_op jit(solution)/shard_map/ppermute | solution.py:11
  33.2 24.6 %collective-permute-start.1 = (bf16[128,4096]{1,0:T(8,128)(2,1)S(1)}, bf16[128,4096]{1,0:T(8,128)(2,1)S(1)}, u32[]{:S(2)}, u32[]{:S(2)}) collective-permute-start(bf16[128,4096]{1,0:T(8,128)(2,1)S(1)} %collective-permute-done), channel_id=1, source_target_pairs={{0,8},{8,16},{16,24},{24,0},{1,9},{9,17},{17,25},{25,1},{2,10},{10... | collective-permute-start | bytes 3145736 | tf_op jit(solution)/shard_map/ppermute | solution.py:11
  57.8 24.3 %collective-permute-start.2 = (bf16[128,4096]{1,0:T(8,128)(2,1)S(1)}, bf16[128,4096]{1,0:T(8,128)(2,1)}, u32[]{:S(2)}, u32[]{:S(2)}) collective-permute-start(bf16[128,4096]{1,0:T(8,128)(2,1)S(1)} %collective-permute-done.1), channel_id=1, source_target_pairs={{0,8},{8,16},{16,24},{24,0},{1,9},{9,17},{17,25},{25,1},{2,10},{10... | collective-permute-start | bytes 3145736 | tf_op jit(solution)/shard_map/ppermute | solution.py:11
  197.1 0.7 copy-start.1
  311.4 17.7 %copy-start.2 = (s32[32,128]{1,0:T(8,128)S(1)}, s32[32,128]{1,0:T(8,128)}, u32[]{:S(2)}) copy-start(s32[32,128]{1,0:T(8,128)} %param.11) | copy-start | bytes 49156
  322.2 97.5 %all-to-all-start.1 = ((bf16[32,8,4096]{2,1,0:T(8,128)(2,1)}), bf16[32,8,4096]{2,1,0:T(8,128)(2,1)S(1)}, u32[]{:S(2)}, u32[]{:S(2)}) async-start(bf16[32,8,4096]{2,1,0:T(8,128)(2,1)} %fusion.9), calls=%async_computation.2 | async-start | bytes 4194304 | tf_op jit(solution)/shard_map/all_to_all | solution.py:80
Sparse Core Ops, SparseCore 0:
  9.2 55.9 all-gather.5
  67.1 54.3 all-gather.3
  123.5 54.3 all-gather.7
  197.3 233.6 reduce-scatter.1
